TPU v7x, 32 devices: a whole 2x2x4 slice. The times are simulated.
32 devices in a mesh: row: 8 (over z, x), col: 4 (over y, core).
Axes of the slice: x: 2, y: 2, z: 4, core: 2. Of those that a mesh axis runs over, the one named last changes fastest.
Arguments:
- vectors: bfloat16 [4, 4, 8, 16, 256], P(None, 'col', 'row'), may hold values from -6 to 6
- tiles: bfloat16 [8, 4, 64, 256, 256], P('row', 'col'), may hold values from -0.0625 to 0.0625
- tile_coords: int32 [8, 4, 64, 2], P('row', 'col'), may hold values from 0 to 127, as said below
- tile_count: int32 [8, 4], P('row', 'col'), may hold values from 16 to 64, as said below
Outputs:
- product: float32 [4, 4, 8, 16, 256], P(None, 'col', 'row')
Inputs may be any that keep to these rules, and one draw needn't show every extreme that they name: `tile_coords`: for the device in grid row r and grid column c every slot's block row I has I % 8 == r, its block column J has (J // 8) % 4 == c, and J <= I. `tile_count`: counts differ from device to device; in every draw some device uses all 64 slots and some other uses 64 // 4.
All inputs are finite; a program needn't handle non-finite values.
Results may differ from a plain program's by a relative error of at most 0.0003.
Values may be sent and summed in bfloat16 or wider, within the bound.
No kernel may reach another device: no remote copies, remote signals or barrier semaphores. Data moves between devices by JAX's collectives and lax.ppermute only.
A program may use at most 64 MiB of HBM per device.

v0:
```python
import jax
import jax.numpy as jnp
from jax import lax
from jax.sharding import PartitionSpec as P

TILE_GROUP = 8


def body(vectors, tiles, tile_coords, tile_count):
    grid_rows = lax.axis_size("row")
    grid_cols = lax.axis_size("col")
    repeats = vectors.shape[0]
    vec_count = vectors.shape[3]
    tile_width = vectors.shape[4]
    slot_count = tiles.shape[2]
    cells = grid_rows * grid_cols
    local_blocks = vectors.reshape(repeats, 1, vec_count, tile_width)
    column_blocks = lax.all_gather(local_blocks, "row", axis=1, tiled=True).reshape(
        repeats * grid_rows, vec_count, tile_width
    )
    row_blocks = lax.all_gather(local_blocks, "col", axis=1, tiled=True).reshape(
        repeats * grid_cols, vec_count, tile_width
    )
    matrices_all = tiles.reshape(slot_count, tile_width, tile_width)
    coords_all = tile_coords.reshape(slot_count, 2)
    filled = tile_count.reshape(())
    turns = (filled + TILE_GROUP - 1) // TILE_GROUP
    row_slots = jnp.arange(repeats * grid_cols, dtype=jnp.int32)
    col_slots = jnp.arange(repeats * grid_rows, dtype=jnp.int32)
    group_ids = jnp.arange(TILE_GROUP, dtype=jnp.int32)

    def load_group(turn):
        start = turn * TILE_GROUP
        matrices = lax.dynamic_slice_in_dim(matrices_all, start, TILE_GROUP, 0)
        positions = lax.dynamic_slice_in_dim(coords_all, start, TILE_GROUP, 0)
        active = start + group_ids < filled
        upper_index = positions[:, 0] // cells * grid_cols + positions[:, 0] % cells // grid_rows
        lower_index = positions[:, 1] // cells * grid_rows + positions[:, 1] % grid_rows
        row_hits = jnp.where(
            active[:, None] & (upper_index[:, None] == row_slots[None, :]), 1.0, 0.0
        ).astype(jnp.float32)
        col_hits = jnp.where(
            active[:, None] & (lower_index[:, None] == col_slots[None, :]), 1.0, 0.0
        ).astype(jnp.float32)
        return (matrices, upper_index, lower_index, row_hits, col_hits)

    def forward_add(total, matrices, lower_index, row_hits):
        sources = jnp.take(column_blocks, lower_index, axis=0)
        terms = jnp.einsum("snb,smb->snm", sources, matrices, preferred_element_type=jnp.float32)
        return total + jnp.einsum("su,snm->unm", row_hits, terms, precision=lax.Precision.HIGHEST)

    def mirror_add(total, matrices, upper_index, col_hits):
        targets = jnp.take(row_blocks, upper_index, axis=0)
        terms = jnp.einsum("snb,sbm->snm", targets, matrices, preferred_element_type=jnp.float32)
        return total + jnp.einsum("sv,snm->vnm", col_hits, terms, precision=lax.Precision.HIGHEST)

    row_start = jnp.zeros((repeats * grid_cols, vec_count, tile_width), jnp.float32)
    col_start = jnp.zeros((repeats * grid_rows, vec_count, tile_width), jnp.float32)

    def forward_turn(turn, total):
        matrices, upper_index, lower_index, row_hits, col_hits = load_group(turn)
        return forward_add(total, matrices, lower_index, row_hits)

    def mirror_turn(turn, total):
        matrices, upper_index, lower_index, row_hits, col_hits = load_group(turn)
        return mirror_add(total, matrices, upper_index, col_hits)

    row_acc = lax.fori_loop(0, turns, forward_turn, row_start)
    col_acc = lax.fori_loop(0, turns, mirror_turn, col_start)
    row_terms = row_acc.reshape(repeats, grid_cols, vec_count, tile_width)
    col_terms = col_acc.reshape(repeats, grid_rows, vec_count, tile_width)
    row_whole = lax.psum(row_terms, "col")
    col_whole = lax.psum(col_terms, "row")
    row_mine = lax.dynamic_slice_in_dim(row_whole, lax.axis_index("col"), 1, 1)
    col_mine = lax.dynamic_slice_in_dim(col_whole, lax.axis_index("row"), 1, 1)
    return (row_mine + col_mine).reshape(repeats, 1, 1, vec_count, tile_width)


def solution(mesh):
    return jax.shard_map(
        body,
        mesh=mesh,
        in_specs=(
            P(None, "col", "row", None, None),
            P("row", "col", None, None, None),
            P("row", "col", None, None),
            P("row", "col"),
        ),
        out_specs=P(None, "col", "row", None, None),
        check_vma=False,
    )
```

profile of v0, /device:TPU:0, one launch (start us, length us, event | category | flops | bytes accessed | tf_op | source)
XLA Modules:
  0.0 193.9 jit_solution(9262916242494318244)
XLA Ops:
  7.2 32.8 %all-gather = bf16[4,8,1,16,256]{4,3,2,1,0:T(8,128)(2,1)S(1)} all-gather(bf16[4,1,1,16,256]{4,3,2,1,0:T(8,128)(2,1)} %param.8), channel_id=2, replica_groups=mesh['row'=8,'col'=4] {'row'}, dimensions={1}, use_global_device_ids=true | all-gather | bytes 294912 | tf_op jit(solution)/shard_map/all_gather | solution.py:18
  40.0 16.9 %while.30 = (s32[]{:T(128)}, f32[16,16,256]{2,0,1:T(8,128)S(1)}, s32[]{:T(128)}, s32[]{:T(128)}, s32[64,2]{0,1:T(2,128)}, /*index=5*/bf16[32,16,256]{2,1,0:T(8,1...) while((s32[]{:T(128)}, f32[16,16,256]{2,0,1:T(8,128)S(1)}, ...), condition=%wide.region_1.2_spmd.clone, body=%wide.region_0.1_spmd.clone.sunk | while | flops 23168940 | bytes 2036267 | solution.py:68
  40.0 0.8 constant_dynamic-slice_fusion.4
  40.8 0.6 gather_fusion
  41.4 1.6 fusion.66
  43.0 0.7 fusion.67
  43.7 0.5 convolution_add_fusion.4
  44.3 0.8 constant_dynamic-slice_fusion.4
  45.0 0.6 gather_fusion
  45.6 1.6 fusion.66
  47.2 0.7 fusion.67
  47.9 0.5 convolution_add_fusion.4
  48.5 0.8 constant_dynamic-slice_fusion.4
  49.3 0.6 gather_fusion
  49.8 1.6 fusion.66
  51.5 0.7 fusion.67
  52.7 0.8 constant_dynamic-slice_fusion.4
  53.5 0.6 gather_fusion
  54.0 1.6 fusion.66
  55.7 0.7 fusion.67
  56.3 0.5 convolution_add_fusion.4
  56.9 0.9 copy.5
  57.8 15.6 %all-gather.1 = bf16[4,4,1,16,256]{4,3,2,1,0:T(8,128)(2,1)S(1)} all-gather(bf16[4,1,1,16,256]{4,3,2,1,0:T(8,128)(2,1)S(1)} %copy-done), channel_id=3, replica_groups=mesh['row'=8,'col'=4] {'col'}, dimensions={1}, use_global_device_ids=true | all-gather | bytes 163840 | tf_op jit(solution)/shard_map/all_gather | solution.py:21
  73.5 17.5 %while.31 = (s32[]{:T(128)}, f32[32,16,256]{2,0,1:T(8,128)S(1)}, s32[]{:T(128)}, s32[]{:T(128)}, s32[64,2]{0,1:T(2,128)}, /*index=5*/bf16[16,16,256]{2,1,0:T(8,1...) while((s32[]{:T(128)}, f32[32,16,256]{2,0,1:T(8,128)S(1)}, ...), condition=%wide.region_4.5_spmd.clone, body=%wide.region_3.4_spmd.clone.sunk | while | flops 29526316 | bytes 2560555 | solution.py:69
  73.5 0.8 constant_dynamic-slice_fusion.5
  74.3 0.6 gather_fusion.1
  74.8 1.5 fusion.72
  76.4 0.7 fusion.74
  77.0 0.8 convolution_add_fusion.5
  77.9 0.8 constant_dynamic-slice_fusion.5
  78.7 0.6 gather_fusion.1
  79.2 1.5 fusion.72
  80.8 0.7 fusion.74
  81.4 0.8 convolution_add_fusion.5
  82.2 0.8 constant_dynamic-slice_fusion.5
  83.0 0.6 gather_fusion.1
  83.6 1.5 fusion.72
  85.1 0.7 fusion.74
  85.8 0.8 convolution_add_fusion.5
  86.6 0.8 constant_dynamic-slice_fusion.5
  87.4 0.6 gather_fusion.1
  88.0 1.5 fusion.72
  89.5 0.7 fusion.74
  90.2 0.8 convolution_add_fusion.5
  91.0 1.1 copy.6
  92.1 11.5 %all-reduce.3.cloned.1.call-done = f32[4,4,16,256]{3,2,1,0:T(8,128)} async-done(((f32[4,4,16,256]{3,2,1,0:T(8,128)}), f32[4,4,16,256]{3,2,1,0:T(8,128)}) %all-reduce.3.cloned.1.call-update) | async-done | bytes 262160 | tf_op jit(solution)/shard_map/psum | solution.py:72
  103.6 82.0 %all-reduce.5.cloned.1.call-done = f32[4,8,16,256]{3,2,1,0:T(8,128)} async-done(((f32[4,8,16,256]{3,2,1,0:T(8,128)}), f32[4,8,16,256]{3,2,1,0:T(8,128)}) %all-reduce.5.cloned.1.call-update) | async-done | bytes 524304 | tf_op jit(solution)/shard_map/psum | solution.py:73
  185.6 1.5 add_bitcast_fusion.1
  (33 shorter events, 1.1 us)
Async XLA Ops:
  6.5 51.3 %copy-start = (bf16[4,1,1,16,256]{4,3,2,1,0:T(8,128)(2,1)S(1)}, bf16[4,1,1,16,256]{4,3,2,1,0:T(8,128)(2,1)}, u32[]{:S(2)}) copy-start(bf16[4,1,1,16,256]{4,3,2,1,0:T(8,128)(2,1)} %param.8) | copy-start | bytes 98308
  6.5 97.1 %all-reduce.3.cloned.1.call-start = ((), (), s32[]{:S(2)}) async-start(), calls=%async_computation | async-start | bytes 524288 | tf_op jit(solution)/shard_map/psum | solution.py:72
  57.8 127.8 %all-reduce.5.cloned.1.call-start = ((), (), s32[]{:S(2)}) async-start(), calls=%async_computation.1 | async-start | bytes 1048576 | tf_op jit(solution)/shard_map/psum | solution.py:73
Sparse Core Ops, SparseCore 0:
  57.9 45.6 all-reduce.2
  107.0 78.5 all-reduce.4
where the time goes:
time: 195 us; the launch traced here: 194 us
  waiting for transfers between devices  93.5 us (48%)
  blocking collectives  48.3 us (25%)
  matrix products  17.8 us (9%)
  between operations  14.1 us (7%)
  local copies, waits for them, and re-layouts  12.5 us (6%)
  other arithmetic  7.16 us (4%)
    psum x1, waiting for transfers between devices, body(): col_whole = lax.psum(col_terms, 'row')  82 us
    all_gather x1, blocking collectives, body(): lax.all_gather(local_blocks, 'row', axis=1, tiled=True)  32.8 us
    all_gather x1, blocking collectives, body(): lax.all_gather(local_blocks, 'col', axis=1, tiled=True)  15.6 us
    psum x1, waiting for transfers between devices, body(): row_whole = lax.psum(row_terms, 'col')  11.5 us
    dot_general x4, matrix products, forward_add(): jnp.einsum('snb,smb->snm', sources, matrices, preferred_element_type=jnp....  6.44 us
    dot_general x4, matrix products, mirror_add(): jnp.einsum('snb,sbm->snm', targets, matrices, preferred_element_type=jnp....  6.05 us
    dynamic_slice x8, local copies, waits for them, and re-layouts, load_group(): positions = lax.dynamic_slice_in_dim(coords_all, start, TILE_GROUP, 0)  6.04 us
    lt x8, other arithmetic, load_group(): active = start + group_ids < filled  5.23 us
  transfers between devices with their start and end apart: 2, of which 2 were waited for; matrix products, arithmetic and copies ran while one was open for 9% of the time, Pallas kernels for 0%

commit v1 on v0

--- a/solution.py
+++ b/solution.py
@@ -15,9 +15,10 @@
     slot_count = tiles.shape[2]
     cells = grid_rows * grid_cols
     local_blocks = vectors.reshape(repeats, 1, vec_count, tile_width)
-    column_blocks = lax.all_gather(local_blocks, "row", axis=1, tiled=True).reshape(
-        repeats * grid_rows, vec_count, tile_width
-    )
+    column_blocks = jnp.concatenate(
+        lax.all_to_all(jnp.stack([local_blocks for _ in range(lax.axis_size("row"))]), "row", 0, 0),
+        axis=1,
+    ).reshape(repeats * grid_rows, vec_count, tile_width)
     row_blocks = lax.all_gather(local_blocks, "col", axis=1, tiled=True).reshape(
         repeats * grid_cols, vec_count, tile_width
     )

time: 195 us -> 174 us (0.89)
  blocking collectives: 48.3 us -> 5.63 us
  waiting for transfers between devices: 93.5 us -> 106 us
  starting transfers between devices: 0.04 us -> 7.36 us
    all_gather x1 -> x0, blocking collectives: 32.8 us -> none  [body(): lax.all_gather(local_blocks, 'row', axis=1, tiled=True)]
    psum x1, waiting for transfers between devices: 11.5 us -> 33.8 us  [body(): row_whole = lax.psum(row_terms, 'col')]
    all_gather x1, blocking collectives: 15.6 us -> 5.63 us  [body(): lax.all_gather(local_blocks, 'col', axis=1, tiled=True)]
    psum x1, waiting for transfers between devices: 82 us -> 72 us  [body(): col_whole = lax.psum(col_terms, 'row')]
    all_to_all x0 -> x1, starting transfers between devices: none -> 7.28 us  [body(): lax.all_to_all(jnp.stack([local_blocks for _ in range(lax.axis_size('row'...]
  transfers between devices with their start and end apart: 2 -> 3, of which waited for: 2 -> 2; matrix products, arithmetic and copies ran while one was open for 9% -> 21% of each run, Pallas kernels for 0% -> 0%
where the time goes in v1:
time: 174 us; the launch traced here: 172 us
  waiting for transfers between devices  106 us (61%)
  matrix products  17.8 us (10%)
  between operations  14.1 us (8%)
  local copies, waits for them, and re-layouts  14 us (8%)
  starting transfers between devices  7.36 us (4%)
  other arithmetic  7.16 us (4%)
  blocking collectives  5.63 us (3%)
    psum x1, waiting for transfers between devices, body(): col_whole = lax.psum(col_terms, 'row')  72 us
    psum x1, waiting for transfers between devices, body(): row_whole = lax.psum(row_terms, 'col')  33.8 us
    all_to_all x1, starting transfers between devices, body(): lax.all_to_all(jnp.stack([local_blocks for _ in range(lax.axis_size('row'...  7.28 us
    dot_general x4, matrix products, forward_add(): jnp.einsum('snb,smb->snm', sources, matrices, preferred_element_type=jnp....  6.44 us
    dot_general x4, matrix products, mirror_add(): jnp.einsum('snb,sbm->snm', targets, matrices, preferred_element_type=jnp....  6.04 us
    dynamic_slice x8, local copies, waits for them, and re-layouts, load_group(): positions = lax.dynamic_slice_in_dim(coords_all, start, TILE_GROUP, 0)  6.04 us
    all_gather x1, blocking collectives, body(): lax.all_gather(local_blocks, 'col', axis=1, tiled=True)  5.63 us
    lt x8, other arithmetic, load_group(): active = start + group_ids < filled  5.23 us
  transfers between devices with their start and end apart: 3, of which 2 were waited for; matrix products, arithmetic and copies ran while one was open for 21% of the time, Pallas kernels for 0%

profile of v1, /device:TPU:0, one launch (start us, length us, event | category | flops | bytes accessed | tf_op | source)
XLA Modules:
  0.0 172.4 jit_solution(2892209236763014326)
XLA Ops:
  6.5 1.5 stack.3
  8.0 7.3 %all-to-all-start = ((bf16[8,4,1,16,256]{4,3,1,2,0:T(8,128)(2,1)}), bf16[8,4,1,16,256]{4,3,1,2,0:T(8,128)(2,1)S(1)}, u32[]{:S(2)}, u32[]{:S(2)}) async-start(bf16[8,4,1,16,256]{4,3,1,2,0:T(8,128)(2,1)} %stack.3), calls=%async_computation | async-start | bytes 524288 | tf_op jit(solution)/shard_map/all_to_all | solution.py:19
  16.0 5.6 %all-gather = bf16[4,4,1,16,256]{4,3,2,1,0:T(8,128)(2,1)S(1)} all-gather(bf16[4,1,1,16,256]{4,3,2,1,0:T(8,128)(2,1)} %param.8), channel_id=2, replica_groups=mesh['row'=8,'col'=4] {'col'}, dimensions={1}, use_global_device_ids=true | all-gather | bytes 163840 | tf_op jit(solution)/shard_map/all_gather | solution.py:22
  21.7 17.5 %while.31 = (s32[]{:T(128)}, f32[32,16,256]{2,0,1:T(8,128)S(1)}, s32[]{:T(128)}, s32[]{:T(128)}, s32[64,2]{0,1:T(2,128)}, /*index=5*/bf16[16,16,256]{2,1,0:T(8,1...) while((s32[]{:T(128)}, f32[32,16,256]{2,0,1:T(8,128)S(1)}, ...), condition=%wide.region_4.5_spmd.clone, body=%wide.region_3.4_spmd.clone.sunk | while | flops 29526316 | bytes 2560555 | solution.py:70
  21.7 0.8 constant_dynamic-slice_fusion.5
  22.5 0.6 gather_fusion.1
  23.1 1.5 fusion.72
  24.6 0.7 fusion.74
  25.3 0.8 convolution_add_fusion.5
  26.1 0.8 constant_dynamic-slice_fusion.5
  26.9 0.6 gather_fusion.1
  27.4 1.5 fusion.72
  29.0 0.7 fusion.74
  29.6 0.8 convolution_add_fusion.5
  30.4 0.8 constant_dynamic-slice_fusion.5
  31.2 0.6 gather_fusion.1
  31.8 1.5 fusion.72
  33.3 0.7 fusion.74
  34.0 0.8 convolution_add_fusion.5
  34.8 0.8 constant_dynamic-slice_fusion.5
  35.6 0.6 gather_fusion.1
  36.2 1.5 fusion.72
  37.7 0.7 fusion.74
  38.4 0.8 convolution_add_fusion.5
  39.2 1.1 copy.17
  40.4 16.9 %while.30 = (s32[]{:T(128)}, f32[16,16,256]{2,0,1:T(8,128)S(1)}, s32[]{:T(128)}, s32[]{:T(128)}, s32[64,2]{0,1:T(2,128)}, /*index=5*/bf16[32,16,256]{2,1,0:T(8,1...) while((s32[]{:T(128)}, f32[16,16,256]{2,0,1:T(8,128)S(1)}, ...), condition=%wide.region_1.2_spmd.clone, body=%wide.region_0.1_spmd.clone.sunk | while | flops 23168940 | bytes 2036267 | solution.py:69
  40.4 0.8 constant_dynamic-slice_fusion.4
  41.2 0.6 gather_fusion
  41.8 1.6 fusion.66
  43.4 0.7 fusion.67
  44.7 0.8 constant_dynamic-slice_fusion.4
  45.4 0.6 gather_fusion
  46.0 1.6 fusion.66
  47.6 0.7 fusion.67
  48.3 0.5 convolution_add_fusion.4
  48.9 0.8 constant_dynamic-slice_fusion.4
  49.7 0.6 gather_fusion
  50.2 1.6 fusion.66
  51.9 0.7 fusion.67
  52.5 0.5 convolution_add_fusion.4
  53.1 0.8 constant_dynamic-slice_fusion.4
  53.9 0.6 gather_fusion
  54.4 1.6 fusion.66
  56.1 0.7 fusion.67
  57.3 0.9 copy.16
  58.2 72.0 %all-reduce.5.cloned.1.call-done = f32[4,8,16,256]{3,2,1,0:T(8,128)} async-done(((f32[4,8,16,256]{3,2,1,0:T(8,128)}), f32[4,8,16,256]{3,2,1,0:T(8,128)}) %all-reduce.5.cloned.1.call-update) | async-done | bytes 524304 | tf_op jit(solution)/shard_map/psum | solution.py:74
  130.2 33.8 %all-reduce.3.cloned.1.call-done = f32[4,4,16,256]{3,2,1,0:T(8,128)} async-done(((f32[4,4,16,256]{3,2,1,0:T(8,128)}), f32[4,4,16,256]{3,2,1,0:T(8,128)}) %all-reduce.3.cloned.1.call-update) | async-done | bytes 262160 | tf_op jit(solution)/shard_map/psum | solution.py:73
  164.1 1.5 add_bitcast_fusion.1
  (34 shorter events, 1.7 us)
Async XLA Ops:
  8.0 32.3 %all-to-all-start = ((bf16[8,4,1,16,256]{4,3,1,2,0:T(8,128)(2,1)}), bf16[8,4,1,16,256]{4,3,1,2,0:T(8,128)(2,1)S(1)}, u32[]{:S(2)}, u32[]{:S(2)}) async-start(bf16[8,4,1,16,256]{4,3,1,2,0:T(8,128)(2,1)} %stack.3), calls=%async_computation | async-start | bytes 524288 | tf_op jit(solution)/shard_map/all_to_all | solution.py:19
  15.3 114.9 %all-reduce.5.cloned.1.call-start = ((), (), s32[]{:S(2)}) async-start(), calls=%async_computation.2 | async-start | bytes 1048576 | tf_op jit(solution)/shard_map/psum | solution.py:74
  40.3 123.8 %all-reduce.3.cloned.1.call-start = ((), (), s32[]{:S(2)}) async-start(), calls=%async_computation.1 | async-start | bytes 524288 | tf_op jit(solution)/shard_map/psum | solution.py:73
Sparse Core Ops, SparseCore 0:
  40.4 89.7 all-reduce.4
  132.5 31.4 all-reduce.2
